TPU v7x, 32 devices: a whole 2x2x4 slice. The times are simulated.
32 devices in a mesh: section: 4 (over y, x), coil: 4 (over z), cuts: 2 (over core).
Axes of the slice: x: 2, y: 2, z: 4, core: 2. Of those that a mesh axis runs over, the one named last changes fastest.
Arguments:
- initial: bfloat16 [2, 32, 80, 2, 128], P(None, 'coil', 'cuts'), may hold values from -6 to 6
- sens: bfloat16 [2, 8, 32, 80, 2, 128], P(None, ('coil', 'cuts')), may hold values from -2.5 to 2.5
- kspace: bfloat16 [2, 8, 32, 80, 2, 128], P(None, ('coil', 'cuts')), may hold values from -6 to 6
- mask: int32 [2, 80, 128], replicated, may hold values 0 or 1
- step_sizes: float32 [4], P('section'), may hold values from 0.3 to 1.5
- conv_in: bfloat16 [4, 128, 18], P('section'), may hold values from -1.5 to 1.5
- bias_in: float32 [4, 128], P('section'), may hold values from -3 to 3
- conv_out: bfloat16 [4, 18, 128], P('section'), may hold values from -0.1875 to 0.1875
Outputs:
- cascade_images: bfloat16 [4, 2, 32, 80, 2, 128], P('section', None, 'coil', 'cuts')
Inputs may be any that keep to these rules, and one draw needn't show every extreme that they name: `mask`: 1 marks a sampled phase-encoding line of the slab, 0 one that was not measured.
All inputs are finite; a program needn't handle non-finite values.
Results may differ from a plain program's by a relative error of at most 0.028.
Values may be sent and summed in bfloat16 or wider, within the bound.
No kernel may reach another device: no remote copies, remote signals or barrier semaphores. Data moves between devices by JAX's collectives and lax.ppermute only.
A program may use at most 128 MiB of HBM per device.

v0:
```python
import math
import jax
import jax.numpy as jnp
from jax import lax
from jax.sharding import PartitionSpec as P


def extended_2(x, sides, width):
    for axis, dim in sides:
        size, length = (lax.axis_size(axis), x.shape[dim])
        up = [(i, (i + 1) % size) for i in range(size - 1)]
        down = [(j, i) for i, j in up]
        last = lax.slice_in_dim(x, length - width, length, axis=dim)
        leading = lax.slice_in_dim(x, 0, width, axis=dim)
        before = lax.ppermute(last, axis, up)
        after = lax.ppermute(leading, axis, down)
        x = jnp.concatenate([before, x, after], axis=dim)
    return x


def from_partner(block, axis, bit):
    count = lax.axis_size(axis)
    route = []
    for low in range(count):
        high = low | 1 << bit
        if high != low and high < count:
            route += [(low, high), (high, low)]
    return lax.ppermute(block, axis, route)


def dft_table(length, sign):
    ramp = jnp.arange(length, dtype=jnp.int32)
    phase = ramp[:, None] * ramp[None, :] % length
    angle = phase.astype(jnp.float32) * (2.0 * math.pi / length)
    scale = 1.0 / math.sqrt(length)
    cosine = jnp.cos(angle) * scale
    sine = jnp.sin(angle) * (scale * sign)
    upper = jnp.concatenate([cosine, -sine], axis=1)
    lower = jnp.concatenate([sine, cosine], axis=1)
    return jnp.concatenate([upper, lower], axis=0).astype(jnp.bfloat16)


def pass_last(volume, table):
    shape = volume.shape
    flat = volume.reshape(-1, shape[-2] * shape[-1])
    return (
        jnp.dot(flat, table, preferred_element_type=jnp.float32).astype(jnp.bfloat16).reshape(shape)
    )


def pass_middle(volume, table):
    length = volume.shape[1]
    split = table.reshape(2, length, 2, length)
    return jnp.einsum("pjcz,cjdk->pkdz", volume, split, preferred_element_type=jnp.float32).astype(
        jnp.bfloat16
    )


def pass_first(volume, table):
    length = volume.shape[0]
    split = table.reshape(2, length, 2, length)
    return jnp.einsum("jycz,cjdk->kydz", volume, split, preferred_element_type=jnp.float32).astype(
        jnp.bfloat16
    )


def complex_product(sens, image):
    sens_real = sens[:, :, 0].astype(jnp.float32)
    sens_imag = sens[:, :, 1].astype(jnp.float32)
    image_real = image[:, :, 0].astype(jnp.float32)
    image_imag = image[:, :, 1].astype(jnp.float32)
    return jnp.stack(
        [
            sens_real * image_real - sens_imag * image_imag,
            sens_real * image_imag + sens_imag * image_real,
        ],
        axis=2,
    )


def conj_product(sens, back):
    sens_real = sens[:, :, 0].astype(jnp.float32)
    sens_imag = sens[:, :, 1].astype(jnp.float32)
    back_real = back[:, :, 0].astype(jnp.float32)
    back_imag = back[:, :, 1].astype(jnp.float32)
    return jnp.stack(
        [
            sens_real * back_real + sens_imag * back_imag,
            sens_real * back_imag - sens_imag * back_real,
        ],
        axis=2,
    )


def hidden_layer(extended, out_rows, weights_in, bias):
    width = extended.shape[3]
    padded = jnp.pad(extended, ((0, 0), (0, 0), (0, 0), (1, 1)))
    taps = jnp.stack(
        [
            padded[:, shift_row : shift_row + out_rows, :, shift_col : shift_col + width]
            for shift_row in range(3)
            for shift_col in range(3)
        ],
        axis=2,
    )
    taps = taps.reshape(extended.shape[0], out_rows, 18, width)
    summed = jnp.einsum("hf,xyfz->xyhz", weights_in, taps, preferred_element_type=jnp.float32)
    return jax.nn.silu(summed + bias[None, None, :, None]).astype(jnp.bfloat16)


def combine_taps(beside_all, rows):
    width = beside_all.shape[3]
    padded = jnp.pad(beside_all, ((0, 0), (0, 0), (0, 0), (1, 1)))
    total = jnp.zeros((beside_all.shape[0], rows, 2, width), jnp.float32)
    for shift_row in range(3):
        for shift_col in range(3):
            first = (3 * shift_row + shift_col) * 2
            total = (
                total
                + padded[
                    :,
                    shift_row : shift_row + rows,
                    first : first + 2,
                    shift_col : shift_col + width,
                ]
            )
    return total


def refine_rows(current, weights_in, bias, weights_out):
    rows = current.shape[1]
    extended = extended_2(current, (("cuts", 1),), 1)
    hidden = hidden_layer(extended, rows, weights_in, bias)
    product = jnp.einsum("fh,xyhz->xyfz", weights_out, hidden, preferred_element_type=jnp.float32)
    beside_all = extended_2(product.astype(jnp.bfloat16), (("cuts", 1),), 1).astype(product.dtype)
    return combine_taps(beside_all, rows)


def whole_rows(current):
    return lax.all_gather(current, "cuts", axis=1, tiled=True)


def sum_gradient(back_rows, current):
    mine = lax.psum_scatter(
        back_rows(jnp.int32(0), lax.axis_size("coil") * current.shape[0]).astype(jnp.bfloat16),
        "coil",
        scatter_dimension=0,
        tiled=True,
    )
    grad = lax.psum_scatter(mine, "cuts", scatter_dimension=1, tiled=True).astype(jnp.float32)
    return grad


def finish_step(current, grad, step, weights_in, bias, weights_out):
    refine = refine_rows(current, weights_in, bias, weights_out)
    return (current.astype(jnp.float32) - step * grad + refine).astype(jnp.bfloat16)


def pair_block(current, sens_one, data_one, mask_one, step, weights_in, bias, weights_out, half):
    halves = whole_rows(current)
    whole = lax.all_gather(halves, "coil", axis=0, tiled=True)
    size_x, size_y, _, size_z = whole.shape
    half_x = size_x // 2
    half_y = size_y // 2
    forward_x, forward_y, forward_z = (
        dft_table(size_x, 1.0),
        dft_table(size_y, 1.0),
        dft_table(size_z, 1.0),
    )
    back_x, back_y, back_z = (
        dft_table(size_x, -1.0),
        dft_table(size_y, -1.0),
        dft_table(size_z, -1.0),
    )
    lower_side = half == 0
    x_start = half * half_x
    x_other = (1 - half) * half_x
    y_start = half * half_y
    y_other = (1 - half) * half_y
    rows_in = lax.dynamic_slice_in_dim(whole, x_start, half_x, 0)
    sens_rows = lax.dynamic_slice_in_dim(sens_one, x_start, half_x, 0)
    coil_image = complex_product(sens_rows, rows_in).astype(jnp.bfloat16)
    partial_value = pass_middle(pass_last(coil_image, forward_z), forward_y)
    kept = lax.dynamic_slice_in_dim(partial_value, y_start, half_y, 1)
    sent = lax.dynamic_slice_in_dim(partial_value, y_other, half_y, 1)
    arrived = from_partner(sent, "section", 0)
    assembled = jnp.concatenate(
        [jnp.where(lower_side, kept, arrived), jnp.where(lower_side, arrived, kept)], axis=0
    )
    predicted = pass_first(assembled, forward_x)
    data_half = lax.dynamic_slice_in_dim(data_one, y_start, half_y, 1)
    mask_half = lax.dynamic_slice_in_dim(mask_one, y_start, half_y, 0)
    weight_mask = mask_half.astype(jnp.float32)[None, :, None, :]
    resid = (weight_mask * (data_half.astype(jnp.float32) - predicted.astype(jnp.float32))).astype(
        jnp.bfloat16
    )
    spectrum = pass_first(resid, back_x)
    kept_back = lax.dynamic_slice_in_dim(spectrum, x_start, half_x, 0)
    sent_back = lax.dynamic_slice_in_dim(spectrum, x_other, half_x, 0)
    arrived_back = from_partner(sent_back, "section", 0)
    joined = jnp.concatenate(
        [
            jnp.where(lower_side, kept_back, arrived_back),
            jnp.where(lower_side, arrived_back, kept_back),
        ],
        axis=1,
    )
    back = pass_last(pass_middle(joined, back_y), back_z)
    term = conj_product(sens_rows, back)
    blank = jnp.zeros_like(term)
    full_term = jnp.concatenate(
        [jnp.where(lower_side, term, blank), jnp.where(lower_side, blank, term)], axis=0
    )

    def back_rows(start, count):
        return full_term

    grad = sum_gradient(back_rows, current)
    grad = grad + from_partner(grad.astype(jnp.bfloat16), "section", 0).astype(grad.dtype)
    return finish_step(current, grad, step, weights_in, bias, weights_out)


def body(initial, sens, kspace, mask, step_sizes, conv_in, bias_in, conv_out):
    section_count = lax.axis_size("section")
    position = lax.axis_index("section")
    all_steps, all_bias = (
        lax.all_gather(step_sizes, "section", axis=0, tiled=True),
        lax.all_gather(bias_in, "section", axis=0, tiled=True),
    )
    all_in, all_out = (
        lax.all_gather(conv_in, "section", axis=0, tiled=True),
        lax.all_gather(conv_out, "section", axis=0, tiled=True),
    )
    slab = position // 2
    half = position % 2
    current = lax.dynamic_index_in_dim(initial, slab, 0, keepdims=False)
    sens_one = lax.dynamic_index_in_dim(sens, slab, 0, keepdims=False)[0]
    data_one = lax.dynamic_index_in_dim(kspace, slab, 0, keepdims=False)[0]
    mask_one = lax.dynamic_index_in_dim(mask, slab, 0, keepdims=False)
    images = []
    for cascade in range(section_count):
        current = pair_block(
            current,
            sens_one,
            data_one,
            mask_one,
            all_steps[cascade],
            all_in[cascade],
            all_bias[cascade],
            all_out[cascade],
            half,
        )
        images.append(current)
    stacked = jnp.stack(images, axis=0)[:, None]
    arrived = lax.all_to_all(stacked, "section", split_axis=0, concat_axis=1, tiled=True)
    return arrived[:, ::2]


def solution(mesh):
    return jax.shard_map(
        body,
        mesh=mesh,
        in_specs=(
            P(None, "coil", "cuts", None, None),
            P(None, ("coil", "cuts"), None, None, None, None),
            P(None, ("coil", "cuts"), None, None, None, None),
            P(),
            P("section"),
            P("section", None, None),
            P("section", None),
            P("section", None, None),
        ),
        out_specs=P("section", None, "coil", "cuts", None, None),
        check_vma=False,
    )
```

profile of v0, /device:TPU:0, one launch (start us, length us, event | category | flops | bytes accessed | tf_op | source)
XLA Modules:
  0.0 516.5 jit_solution(3672511079097253560)
XLA Ops:
  12.5 32.9 %all-gather.14.cloned.1.call-done = bf16[1,32,80,2,128]{4,2,3,0,1:T(8,128)(2,1)} async-done(((bf16[1,8,80,2,128]{4,2,3,0,1:T(8,128)(2,1)}), bf16[1,32,80,2,128]{4,2,3,0,1:T(8,128)(2,1)}) %all-gather.14.cloned.1.call-update) | async-done | bytes 1310736 | tf_op jit(solution)/shard_map/all_gather | solution.py:161
  60.5 5.9 %collective-permute-done.1 = bf16[16,40,2,128]{3,1,0,2:T(8,128)(2,1)S(1)} collective-permute-done((bf16[16,40,2,128]{3,1,0,2:T(8,128)(2,1)S(1)}, bf16[16,40,2,128]{3,1,0,2:T(8,128)(2,1)S(1)}, u32[]{:S(2)}, u32[]{:S(2)}) %collective-permute-start.1) | collective-permute-done | bytes 327712 | tf_op jit(solution)/shard_map/ppermute | solution.py:28
  75.5 7.9 %all-gather.2 = f32[4,1,128]{2,1,0:T(1,128)S(1)} all-gather(f32[1,1,128]{2,1,0:T(1,128)S(1)} %bitcast.665), channel_id=1, replica_groups=mesh['section'=4,'coil'=4,'cuts'=2] {'section'}, dimensions={0}, use_global_device_ids=true | all-gather | bytes 2560 | tf_op jit(solution)/shard_map/all_gather | solution.py:228
  83.4 8.1 %all_gather.39 = bf16[4,128,18]{1,2,0:T(8,128)(2,1)S(1)} all-gather(bf16[1,128,18]{1,2,0:T(8,128)(2,1)S(1)} %copy-done.37), channel_id=1, replica_groups=mesh['section'=4,'coil'=4,'cuts'=2] {'section'}, dimensions={0}, use_global_device_ids=true | all-gather | bytes 23040 | tf_op jit(solution)/shard_map/all_gather | solution.py:231
  91.5 8.9 %all-reduce.8 = f32[4]{0:T(128)S(1)} all-reduce(f32[4]{0:T(128)S(1)} %dynamic-update-slice), channel_id=1, replica_groups=mesh['section'=4,'coil'=4,'cuts'=2] {'section'}, use_global_device_ids=true, to_apply=%add.8 | all-reduce | flops 4 | bytes 32
  100.4 7.4 %all_gather.41 = bf16[4,18,128]{2,1,0:T(8,128)(2,1)S(1)} all-gather(bf16[1,18,128]{2,1,0:T(8,128)(2,1)S(1)} %copy-done.38), channel_id=1, replica_groups=mesh['section'=4,'coil'=4,'cuts'=2] {'section'}, dimensions={0}, use_global_device_ids=true | all-gather | bytes 23040 | tf_op jit(solution)/shard_map/all_gather | solution.py:232
  113.5 10.2 %convert_bitcast_fusion.3 = bf16[8,40,18,128]{3,2,1,0:T(8,128)(2,1)S(1)} fusion(f32[128]{0:T(128)S(1)} %get-tuple-element.73, bf16[8,40,18,128]{3,1,2,0:T(8,128)(2,1)} %bitcast.650, bf16[4,18,128]{2,1,0:T(8,128)(2,1)S(1)} %all_gather.41, bf16[4,128,18]{1,2,0:T(8,128)(2,1)S(1)} %all_gather.39), kind=kOutput, calls=%fused_computation.111 | convolution fusion | flops 409681920 | bytes 2961920 | tf_op jit(solution)/shard_map/fh,xyhz->xyfz/dot_general | solution.py:134
  141.1 32.4 %all-gather.8.cloned.1.call-done = bf16[32,80,2,128]{3,1,2,0:T(8,128)(2,1)} async-done(((bf16[8,80,2,128]{3,1,2,0:T(8,128)(2,1)}), bf16[32,80,2,128]{3,1,2,0:T(8,128)(2,1)}) %all-gather.8.cloned.1.call-update) | async-done | bytes 1310736 | tf_op jit(solution)/shard_map/all_gather | solution.py:161
  178.1 7.3 %collective-permute-done.7 = bf16[16,40,2,128]{3,1,0,2:T(8,128)(2,1)S(1)} collective-permute-done((bf16[16,40,2,128]{3,1,0,2:T(8,128)(2,1)S(1)}, bf16[16,40,2,128]{3,1,0,2:T(8,128)(2,1)S(1)}, u32[]{:S(2)}, u32[]{:S(2)}) %collective-permute-start.7) | collective-permute-done | bytes 327712 | tf_op jit(solution)/shard_map/ppermute | solution.py:28
  188.3 6.4 %collective-permute-done.8 = bf16[16,40,2,128]{3,1,0,2:T(8,128)(2,1)S(1)} collective-permute-done((bf16[16,40,2,128]{3,1,0,2:T(8,128)(2,1)S(1)}, bf16[16,40,2,128]{3,1,0,2:T(8,128)(2,1)S(1)}, u32[]{:S(2)}, u32[]{:S(2)}) %collective-permute-start.8) | collective-permute-done | bytes 327712 | tf_op jit(solution)/shard_map/ppermute | solution.py:28
  207.1 24.2 %reduce-scatter.13.cloned.1.call-done = bf16[8,80,2,128]{3,1,2,0:T(8,128)(2,1)} async-done(((bf16[32,80,2,128]{3,1,2,0:T(8,128)(2,1)}), bf16[8,80,2,128]{3,1,2,0:T(8,128)(2,1)}) %reduce-scatter.13.cloned.1.call-update) | async-done | bytes 327696 | tf_op jit(solution)/shard_map/reduce_scatter | solution.py:144
  233.1 10.2 %convert_bitcast_fusion.2 = bf16[8,40,18,128]{3,2,1,0:T(8,128)(2,1)S(1)} fusion(f32[128]{0:T(128)S(1)} %get-tuple-element.75, bf16[8,40,18,128]{3,1,2,0:T(8,128)(2,1)} %bitcast.651, bf16[4,18,128]{2,1,0:T(8,128)(2,1)} %copy-done.32, bf16[4,128,18]{1,2,0:T(8,128)(2,1)} %copy-done.31), kind=kOutput, calls=%fused_computation.110 | convolution fusion | flops 409681920 | bytes 2961920 | tf_op jit(solution)/shard_map/fh,xyhz->xyfz/dot_general | solution.py:134
  260.2 31.6 %all-gather.10.cloned.1.call-done = bf16[32,80,2,128]{3,1,2,0:T(8,128)(2,1)} async-done(((bf16[8,80,2,128]{3,1,2,0:T(8,128)(2,1)}), bf16[32,80,2,128]{3,1,2,0:T(8,128)(2,1)}) %all-gather.10.cloned.1.call-update) | async-done | bytes 1310736 | tf_op jit(solution)/shard_map/all_gather | solution.py:161
  296.4 7.3 %collective-permute-done.14 = bf16[16,40,2,128]{3,1,0,2:T(8,128)(2,1)S(1)} collective-permute-done((bf16[16,40,2,128]{3,1,0,2:T(8,128)(2,1)S(1)}, bf16[16,40,2,128]{3,1,0,2:T(8,128)(2,1)S(1)}, u32[]{:S(2)}, u32[]{:S(2)}) %collective-permute-start.14) | collective-permute-done | bytes 327712 | tf_op jit(solution)/shard_map/ppermute | solution.py:28
  306.6 6.4 %collective-permute-done.15 = bf16[16,40,2,128]{3,1,0,2:T(8,128)(2,1)S(1)} collective-permute-done((bf16[16,40,2,128]{3,1,0,2:T(8,128)(2,1)S(1)}, bf16[16,40,2,128]{3,1,0,2:T(8,128)(2,1)S(1)}, u32[]{:S(2)}, u32[]{:S(2)}) %collective-permute-start.15) | collective-permute-done | bytes 327712 | tf_op jit(solution)/shard_map/ppermute | solution.py:28
  325.4 24.1 %reduce-scatter.17.cloned.1.call-done = bf16[8,80,2,128]{3,1,2,0:T(8,128)(2,1)} async-done(((bf16[32,80,2,128]{3,1,2,0:T(8,128)(2,1)}), bf16[8,80,2,128]{3,1,2,0:T(8,128)(2,1)}) %reduce-scatter.17.cloned.1.call-update) | async-done | bytes 327696 | tf_op jit(solution)/shard_map/reduce_scatter | solution.py:144
  351.6 10.2 %convert_bitcast_fusion.1 = bf16[8,40,18,128]{3,2,1,0:T(8,128)(2,1)S(1)} fusion(f32[128]{0:T(128)S(1)} %get-tuple-element.74, bf16[8,40,18,128]{3,1,2,0:T(8,128)(2,1)} %bitcast.652, bf16[4,18,128]{2,1,0:T(8,128)(2,1)} %copy-done.32, bf16[4,128,18]{1,2,0:T(8,128)(2,1)} %copy-done.31), kind=kOutput, calls=%fused_computation.109 | convolution fusion | flops 409681920 | bytes 2961920 | tf_op jit(solution)/shard_map/fh,xyhz->xyfz/dot_general | solution.py:134
  367.6 5.0 collective-permute-done.16
  378.2 31.6 %all-gather.12.cloned.1.call-done = bf16[32,80,2,128]{3,1,2,0:T(8,128)(2,1)} async-done(((bf16[8,80,2,128]{3,1,2,0:T(8,128)(2,1)}), bf16[32,80,2,128]{3,1,2,0:T(8,128)(2,1)}) %all-gather.12.cloned.1.call-update) | async-done | bytes 1310736 | tf_op jit(solution)/shard_map/all_gather | solution.py:161
  414.4 7.3 %collective-permute-done.21 = bf16[16,40,2,128]{3,1,0,2:T(8,128)(2,1)S(1)} collective-permute-done((bf16[16,40,2,128]{3,1,0,2:T(8,128)(2,1)S(1)}, bf16[16,40,2,128]{3,1,0,2:T(8,128)(2,1)S(1)}, u32[]{:S(2)}, u32[]{:S(2)}) %collective-permute-start.21) | collective-permute-done | bytes 327712 | tf_op jit(solution)/shard_map/ppermute | solution.py:28
  424.6 6.4 %collective-permute-done.22 = bf16[16,40,2,128]{3,1,0,2:T(8,128)(2,1)S(1)} collective-permute-done((bf16[16,40,2,128]{3,1,0,2:T(8,128)(2,1)S(1)}, bf16[16,40,2,128]{3,1,0,2:T(8,128)(2,1)S(1)}, u32[]{:S(2)}, u32[]{:S(2)}) %collective-permute-start.22) | collective-permute-done | bytes 327712 | tf_op jit(solution)/shard_map/ppermute | solution.py:28
  443.4 24.2 %reduce-scatter.21.cloned.1.call-done = bf16[8,80,2,128]{3,1,2,0:T(8,128)(2,1)} async-done(((bf16[32,80,2,128]{3,1,2,0:T(8,128)(2,1)}), bf16[8,80,2,128]{3,1,2,0:T(8,128)(2,1)}) %reduce-scatter.21.cloned.1.call-update) | async-done | bytes 327696 | tf_op jit(solution)/shard_map/reduce_scatter | solution.py:144
  469.4 10.2 %convert_bitcast_fusion = bf16[8,40,18,128]{3,2,1,0:T(8,128)(2,1)S(1)} fusion(f32[128]{0:T(128)S(1)} %get-tuple-element.76, bf16[8,40,18,128]{3,1,2,0:T(8,128)(2,1)} %bitcast.649, bf16[4,18,128]{2,1,0:T(8,128)(2,1)} %copy-done.32, bf16[4,128,18]{1,2,0:T(8,128)(2,1)} %copy-done.31), kind=kOutput, calls=%fused_computation.108 | convolution fusion | flops 409681920 | bytes 2961920 | tf_op jit(solution)/shard_map/fh,xyhz->xyfz/dot_general | solution.py:134
  494.6 13.7 %all_to_all.12 = bf16[4,1,8,40,2,128]{5,4,3,2,1,0:T(2,128)(2,1)S(1)} all-to-all(bf16[4,1,8,40,2,128]{5,4,3,2,1,0:T(2,128)(2,1)S(1)} %maximum_bitcast_fusion), channel_id=1, replica_groups=mesh['section'=4,'coil'=4,'cuts'=2] {'section'}, dimensions={0} | all-to-all | bytes 1310720 | tf_op jit(solution)/shard_map/all_to_all | solution.py:255
  (356 shorter events, 160.2 us)
Async XLA Ops:
  6.5 38.8 %all-gather.14.cloned.1.call-start = ((), (), s32[]{:S(2)}) async-start(), calls=%async_computation.20 | async-start | bytes 1638400 | tf_op jit(solution)/shard_map/all_gather | solution.py:161
  10.1 101.5 %reduce-scatter.9.cloned.1.call-start = ((), (), s32[]{:S(2)}) async-start(), calls=%async_computation.9 | async-start | bytes 1638400 | tf_op jit(solution)/shard_map/reduce_scatter | solution.py:144
  48.3 8.8 %collective-permute-start = (bf16[16,40,2,128]{3,1,0,2:T(8,128)(2,1)S(1)}, bf16[16,40,2,128]{3,1,0,2:T(8,128)(2,1)S(1)}, u32[]{:S(2)}, u32[]{:S(2)}) collective-permute-start(bf16[16,40,2,128]{3,1,0,2:T(8,128)(2,1)S(1)} %dynamic-slice_bitcast_fusion.8), channel_id=1, source_target_pairs={{0,8},{8,0},{16,24},{24,16},{1,9},{9,1},{17,25},{25,17},{2,10},{10... | collective-permute-start | bytes 983048 | tf_op jit(solution)/shard_map/ppermute | solution.py:28
  58.4 8.0 %collective-permute-start.1 = (bf16[16,40,2,128]{3,1,0,2:T(8,128)(2,1)S(1)}, bf16[16,40,2,128]{3,1,0,2:T(8,128)(2,1)S(1)}, u32[]{:S(2)}, u32[]{:S(2)}) collective-permute-start(bf16[16,40,2,128]{3,1,0,2:T(8,128)(2,1)S(1)} %dynamic-slice_bitcast_fusion.7), channel_id=1, source_target_pairs={{0,8},{8,0},{16,24},{24,16},{1,9},{9,1},{17,25},{25,17},{2,10},{10... | collective-permute-start | bytes 983048 | tf_op jit(solution)/shard_map/ppermute | solution.py:28
  70.7 56.7 %reduce-scatter.11.cloned.1.call-start = ((), (), s32[]{:S(2)}) async-start(), calls=%async_computation.10 | async-start | bytes 491520 | tf_op jit(solution)/shard_map/reduce_scatter | solution.py:150
  70.9 37.0 %collective-permute-start.3 = (bf16[8,1,2,128]{3,2,1,0:T(2,128)(2,1)S(1)}, bf16[8,1,2,128]{3,2,1,0:T(2,128)(2,1)S(1)}, u32[]{:S(2)}, u32[]{:S(2)}) collective-permute-start(bf16[8,1,2,128]{3,2,1,0:T(2,128)(2,1)S(1)} %get-tuple-element.67), channel_id=1, source_target_pairs={{0,1},{2,3},{4,5},{6,7},{8,9},{10,11},{12,13},{14,15},{16,17},{18,... | collective-permute-start | bytes 12296 | tf_op jit(solution)/shard_map/ppermute | solution.py:15
  72.2 35.7 %collective-permute-start.4 = (bf16[8,1,2,128]{3,2,1,0:T(2,128)(2,1)S(1)}, bf16[8,1,2,128]{3,2,1,0:T(2,128)(2,1)S(1)}, u32[]{:S(2)}, u32[]{:S(2)}) collective-permute-start(bf16[8,1,2,128]{3,2,1,0:T(2,128)(2,1)S(1)} %get-tuple-element.68), channel_id=1, source_target_pairs={{1,0},{3,2},{5,4},{7,6},{9,8},{11,10},{13,12},{15,14},{17,16},{19,... | collective-permute-start | bytes 12296 | tf_op jit(solution)/shard_map/ppermute | solution.py:16
  113.4 60.1 %all-gather.8.cloned.1.call-start = ((), (), s32[]{:S(2)}) async-start(), calls=%async_computation.11 | async-start | bytes 1638400 | tf_op jit(solution)/shard_map/all_gather | solution.py:161
  141.1 90.2 %reduce-scatter.13.cloned.1.call-start = ((), (), s32[]{:S(2)}) async-start(), calls=%async_computation.12 | async-start | bytes 1638400 | tf_op jit(solution)/shard_map/reduce_scatter | solution.py:144
  176.6 8.8 %collective-permute-start.7 = (bf16[16,40,2,128]{3,1,0,2:T(8,128)(2,1)S(1)}, bf16[16,40,2,128]{3,1,0,2:T(8,128)(2,1)S(1)}, u32[]{:S(2)}, u32[]{:S(2)}) collective-permute-start(bf16[16,40,2,128]{3,1,0,2:T(8,128)(2,1)S(1)} %dynamic-slice_bitcast_fusion.6), channel_id=1, source_target_pairs={{0,8},{8,0},{16,24},{24,16},{1,9},{9,1},{17,25},{25,17},{2,10},{10... | collective-permute-start | bytes 983048 | tf_op jit(solution)/shard_map/ppermute | solution.py:28
  186.8 7.9 %collective-permute-start.8 = (bf16[16,40,2,128]{3,1,0,2:T(8,128)(2,1)S(1)}, bf16[16,40,2,128]{3,1,0,2:T(8,128)(2,1)S(1)}, u32[]{:S(2)}, u32[]{:S(2)}) collective-permute-start(bf16[16,40,2,128]{3,1,0,2:T(8,128)(2,1)S(1)} %dynamic-slice_bitcast_fusion.5), channel_id=1, source_target_pairs={{0,8},{8,0},{16,24},{24,16},{1,9},{9,1},{17,25},{25,17},{2,10},{10... | collective-permute-start | bytes 983048 | tf_op jit(solution)/shard_map/ppermute | solution.py:28
  199.0 47.5 %reduce-scatter.15.cloned.1.call-start = ((), (), s32[]{:S(2)}) async-start(), calls=%async_computation.13 | async-start | bytes 491520 | tf_op jit(solution)/shard_map/reduce_scatter | solution.py:150
  233.1 58.7 %all-gather.10.cloned.1.call-start = ((), (), s32[]{:S(2)}) async-start(), calls=%async_computation.14 | async-start | bytes 1638400 | tf_op jit(solution)/shard_map/all_gather | solution.py:161
  247.6 7.0 %collective-permute-start.9 = (bf16[8,40,2,128]{3,2,1,0:T(2,128)(2,1)S(1)}, bf16[8,40,2,128]{3,2,1,0:T(2,128)(2,1)S(1)}, u32[]{:S(2)}, u32[]{:S(2)}) collective-permute-start(bf16[8,40,2,128]{3,2,1,0:T(2,128)(2,1)S(1)} %copy.190), channel_id=1, source_target_pairs={{0,8},{8,0},{16,24},{24,16},{1,9},{9,1},{17,25},{25,17},{2,10},{10... | collective-permute-start | bytes 491528 | tf_op jit(solution)/shard_map/ppermute | solution.py:28
  260.1 89.4 %reduce-scatter.17.cloned.1.call-start = ((), (), s32[]{:S(2)}) async-start(), calls=%async_computation.15 | async-start | bytes 1638400 | tf_op jit(solution)/shard_map/reduce_scatter | solution.py:144
  294.9 8.8 %collective-permute-start.14 = (bf16[16,40,2,128]{3,1,0,2:T(8,128)(2,1)S(1)}, bf16[16,40,2,128]{3,1,0,2:T(8,128)(2,1)S(1)}, u32[]{:S(2)}, u32[]{:S(2)}) collective-permute-start(bf16[16,40,2,128]{3,1,0,2:T(8,128)(2,1)S(1)} %dynamic-slice_bitcast_fusion.4), channel_id=1, source_target_pairs={{0,8},{8,0},{16,24},{24,16},{1,9},{9,1},{17,25},{25,17},{2,10},{10... | collective-permute-start | bytes 983048 | tf_op jit(solution)/shard_map/ppermute | solution.py:28
  305.1 8.0 %collective-permute-start.15 = (bf16[16,40,2,128]{3,1,0,2:T(8,128)(2,1)S(1)}, bf16[16,40,2,128]{3,1,0,2:T(8,128)(2,1)S(1)}, u32[]{:S(2)}, u32[]{:S(2)}) collective-permute-start(bf16[16,40,2,128]{3,1,0,2:T(8,128)(2,1)S(1)} %dynamic-slice_bitcast_fusion.3), channel_id=1, source_target_pairs={{0,8},{8,0},{16,24},{24,16},{1,9},{9,1},{17,25},{25,17},{2,10},{10... | collective-permute-start | bytes 983048 | tf_op jit(solution)/shard_map/ppermute | solution.py:28
  317.3 47.3 %reduce-scatter.19.cloned.1.call-start = ((), (), s32[]{:S(2)}) async-start(), calls=%async_computation.16 | async-start | bytes 491520 | tf_op jit(solution)/shard_map/reduce_scatter | solution.py:150
  351.4 58.5 %all-gather.12.cloned.1.call-start = ((), (), s32[]{:S(2)}) async-start(), calls=%async_computation.17 | async-start | bytes 1638400 | tf_op jit(solution)/shard_map/all_gather | solution.py:161
  365.6 7.0 %collective-permute-start.16 = (bf16[8,40,2,128]{3,2,1,0:T(2,128)(2,1)S(1)}, bf16[8,40,2,128]{3,2,1,0:T(2,128)(2,1)S(1)}, u32[]{:S(2)}, u32[]{:S(2)}) collective-permute-start(bf16[8,40,2,128]{3,2,1,0:T(2,128)(2,1)S(1)} %copy.210), channel_id=1, source_target_pairs={{0,8},{8,0},{16,24},{24,16},{1,9},{9,1},{17,25},{25,17},{2,10},{10... | collective-permute-start | bytes 491528 | tf_op jit(solution)/shard_map/ppermute | solution.py:28
  378.1 89.4 %reduce-scatter.21.cloned.1.call-start = ((), (), s32[]{:S(2)}) async-start(), calls=%async_computation.18 | async-start | bytes 1638400 | tf_op jit(solution)/shard_map/reduce_scatter | solution.py:144
  412.9 8.8 %collective-permute-start.21 = (bf16[16,40,2,128]{3,1,0,2:T(8,128)(2,1)S(1)}, bf16[16,40,2,128]{3,1,0,2:T(8,128)(2,1)S(1)}, u32[]{:S(2)}, u32[]{:S(2)}) collective-permute-start(bf16[16,40,2,128]{3,1,0,2:T(8,128)(2,1)S(1)} %dynamic-slice_bitcast_fusion.2), channel_id=1, source_target_pairs={{0,8},{8,0},{16,24},{24,16},{1,9},{9,1},{17,25},{25,17},{2,10},{10... | collective-permute-start | bytes 983048 | tf_op jit(solution)/shard_map/ppermute | solution.py:28
  423.1 7.9 %collective-permute-start.22 = (bf16[16,40,2,128]{3,1,0,2:T(8,128)(2,1)S(1)}, bf16[16,40,2,128]{3,1,0,2:T(8,128)(2,1)S(1)}, u32[]{:S(2)}, u32[]{:S(2)}) collective-permute-start(bf16[16,40,2,128]{3,1,0,2:T(8,128)(2,1)S(1)} %dynamic-slice_bitcast_fusion.1), channel_id=1, source_target_pairs={{0,8},{8,0},{16,24},{24,16},{1,9},{9,1},{17,25},{25,17},{2,10},{10... | collective-permute-start | bytes 983048 | tf_op jit(solution)/shard_map/ppermute | solution.py:28
  435.3 47.3 %reduce-scatter.23.cloned.1.call-start = ((), (), s32[]{:S(2)}) async-start(), calls=%async_computation.19 | async-start | bytes 491520 | tf_op jit(solution)/shard_map/reduce_scatter | solution.py:150
  (57 other events, 394.8 us)
Sparse Core Ops, SparseCore 0:
  10.2 35.1 all-gather.13
  70.8 32.0 reduce-scatter.8
  113.6 7.5 reduce-scatter.10
  141.2 32.3 all-gather.7
  199.1 32.1 reduce-scatter.12
  233.3 6.4 reduce-scatter.14
  260.2 31.5 all-gather.9
  317.4 32.0 reduce-scatter.16
  351.8 6.4 reduce-scatter.18
  378.3 31.5 all-gather.11
  435.4 32.1 reduce-scatter.20
  469.6 6.4 reduce-scatter.22
where the time goes:
time: 525 us; the launch traced here: 516 us
  waiting for transfers between devices  278 us (53%)
  blocking collectives  54.4 us (10%)
  matrix products  49.7 us (9%)
  local copies, waits for them, and re-layouts  44.4 us (8%)
  starting transfers between devices  41.4 us (8%)
  other arithmetic  32.6 us (6%)
  between operations  16.4 us (3%)
    all_gather x4, waiting for transfers between devices, pair_block(): whole = lax.all_gather(halves, 'coil', axis=0, tiled=True)  129 us
    reduce_scatter x4, waiting for transfers between devices, sum_gradient(): lax.psum_scatter(back_rows(jnp.int32(0), lax.axis_size('coil') * current....  72.5 us
    ppermute x12, waiting for transfers between devices, from_partner(): return lax.ppermute(block, axis, route)  71.4 us
    dot_general x4, matrix products, refine_rows(): jnp.einsum('fh,xyhz->xyfz', weights_out, hidden, preferred_element_type=j...  40.9 us
    ppermute x12, starting transfers between devices, from_partner(): return lax.ppermute(block, axis, route)  18.4 us
    all_to_all x1, blocking collectives, body(): lax.all_to_all(stacked, 'section', split_axis=0, concat_axis=1, tiled=True)  13.7 us
    ppermute x8, starting transfers between devices, extended_2(): after = lax.ppermute(leading, axis, down)  11.8 us
    ppermute x8, starting transfers between devices, extended_2(): before = lax.ppermute(last, axis, up)  10.5 us
  transfers between devices with their start and end apart: 40, of which 22 were waited for; matrix products, arithmetic and copies ran while one was open for 13% of the time, Pallas kernels for 0%

commit v1 on v0

--- a/solution.py
+++ b/solution.py
@@ -3,6 +3,19 @@
 import jax.numpy as jnp
 from jax import lax
 from jax.sharding import PartitionSpec as P
+
+
+def ring_gather(x, axis, dim):
+    ways = lax.axis_size(axis)
+    up = [(d, (d + 1) % ways) for d in range(ways)]
+    down = [(d, (d - 1) % ways) for d in range(ways)]
+    earlier, later = ([x], [x])
+    for _ in range(ways // 2):
+        earlier.append(lax.ppermute(earlier[-1], axis, up))
+    for _ in range((ways - 1) // 2):
+        later.append(lax.ppermute(later[-1], axis, down))
+    line = jnp.concatenate([*earlier[::-1], *later[1:]], axis=dim)
+    return jnp.roll(line, (lax.axis_index(axis) - ways // 2) * x.shape[dim], axis=dim)
 
 
 def extended_2(x, sides, width):
@@ -158,7 +171,7 @@
 
 def pair_block(current, sens_one, data_one, mask_one, step, weights_in, bias, weights_out, half):
     halves = whole_rows(current)
-    whole = lax.all_gather(halves, "coil", axis=0, tiled=True)
+    whole = ring_gather(halves, "coil", 0)
     size_x, size_y, _, size_z = whole.shape
     half_x = size_x // 2
     half_y = size_y // 2

time: 525 us -> 496 us (0.945)
  waiting for transfers between devices: 278 us -> 230 us
  starting transfers between devices: 41.4 us -> 59.2 us
  other arithmetic: 32.6 us -> 26.6 us
    all_gather x4 -> x0, waiting for transfers between devices: 129 us -> none  [pair_block(): whole = lax.all_gather(halves, 'coil', axis=0, tiled=True)]
    ppermute x0 -> x12, waiting for transfers between devices: none -> 87 us  [the longest x8 74.6 us: ring_gather(): earlier.append(lax.ppermute(earlier[-1], axis, up))]
    ppermute x0 -> x12, starting transfers between devices: none -> 18.7 us  [the longest x4 16.4 us: ring_gather(): later.append(lax.ppermute(later[-1], axis, down))]
    dot_general x0 -> x4, local copies, waits for them, and re-layouts: none -> 6.95 us  [refine_rows(): jnp.einsum('fh,xyhz->xyfz', weights_out, hidden, preferred_element_type=j...]
  transfers between devices with their start and end apart: 40 -> 48, of which waited for: 22 -> 29; matrix products, arithmetic and copies ran while one was open for 13% -> 16% of each run, Pallas kernels for 0% -> 0%
where the time goes in v1:
time: 496 us; the launch traced here: 487 us
  waiting for transfers between devices  230 us (46%)
  starting transfers between devices  59.2 us (12%)
  blocking collectives  54.5 us (11%)
  matrix products  54 us (11%)
  local copies, waits for them, and re-layouts  46.6 us (9%)
  other arithmetic  26.6 us (5%)
  between operations  16.3 us (3%)
    ppermute x8, waiting for transfers between devices, ring_gather(): earlier.append(lax.ppermute(earlier[-1], axis, up))  74.6 us
    ppermute x12, waiting for transfers between devices, from_partner(): return lax.ppermute(block, axis, route)  69.4 us
    reduce_scatter x4, waiting for transfers between devices, sum_gradient(): lax.psum_scatter(back_rows(jnp.int32(0), lax.axis_size('coil') * current....  68 us
    dot_general x4, matrix products, refine_rows(): jnp.einsum('fh,xyhz->xyfz', weights_out, hidden, preferred_element_type=j...  45.2 us
    ppermute x12, starting transfers between devices, from_partner(): return lax.ppermute(block, axis, route)  18.4 us
    ppermute x4, starting transfers between devices, ring_gather(): later.append(lax.ppermute(later[-1], axis, down))  16.4 us
    all_to_all x1, blocking collectives, body(): lax.all_to_all(stacked, 'section', split_axis=0, concat_axis=1, tiled=True)  13.8 us
    ppermute x4, waiting for transfers between devices, ring_gather(): later.append(lax.ppermute(later[-1], axis, down))  12.4 us
  transfers between devices with their start and end apart: 48, of which 29 were waited for; matrix products, arithmetic and copies ran while one was open for 16% of the time, Pallas kernels for 0%

profile of v1, /device:TPU:0, one launch (start us, length us, event | category | flops | bytes accessed | tf_op | source)
XLA Modules:
  0.0 486.8 jit_solution(6343493376962927894)
XLA Ops:
  16.6 13.6 %collective-permute-done = bf16[8,80,2,128]{3,1,2,0:T(8,128)(2,1)} collective-permute-done((bf16[8,80,2,128]{3,1,2,0:T(8,128)(2,1)S(1)}, bf16[8,80,2,128]{3,1,2,0:T(8,128)(2,1)}, u32[]{:S(2)}, u32[]{:S(2)}) %collective-permute-start) | collective-permute-done | bytes 327712 | tf_op jit(solution)/shard_map/ppermute | solution.py:14
  32.5 8.6 %collective-permute-done.1 = bf16[8,80,2,128]{3,1,2,0:T(8,128)(2,1)S(1)} collective-permute-done((bf16[8,80,2,128]{3,1,2,0:T(8,128)(2,1)}, bf16[8,80,2,128]{3,1,2,0:T(8,128)(2,1)S(1)}, u32[]{:S(2)}, u32[]{:S(2)}) %collective-permute-start.1) | collective-permute-done | bytes 327712 | tf_op jit(solution)/shard_map/ppermute | solution.py:14
  70.5 7.9 %all-gather.1 = f32[4,1,128]{2,1,0:T(1,128)S(1)} all-gather(f32[1,1,128]{2,1,0:T(1,128)S(1)} %bitcast.673), channel_id=1, replica_groups=mesh['section'=4,'coil'=4,'cuts'=2] {'section'}, dimensions={0}, use_global_device_ids=true | all-gather | bytes 2560 | tf_op jit(solution)/shard_map/all_gather | solution.py:241
  79.0 8.1 %all_gather.26 = bf16[4,128,18]{1,2,0:T(8,128)(2,1)S(1)} all-gather(bf16[1,128,18]{1,2,0:T(8,128)(2,1)S(1)} %copy-done.24), channel_id=1, replica_groups=mesh['section'=4,'coil'=4,'cuts'=2] {'section'}, dimensions={0}, use_global_device_ids=true | all-gather | bytes 23040 | tf_op jit(solution)/shard_map/all_gather | solution.py:244
  87.2 8.9 %all-reduce.8 = f32[4]{0:T(128)S(1)} all-reduce(f32[4]{0:T(128)S(1)} %dynamic-update-slice), channel_id=1, replica_groups=mesh['section'=4,'coil'=4,'cuts'=2] {'section'}, use_global_device_ids=true, to_apply=%add.8 | all-reduce | flops 4 | bytes 32
  96.1 7.4 %all_gather.28 = bf16[4,18,128]{2,1,0:T(8,128)(2,1)S(1)} all-gather(bf16[1,18,128]{2,1,0:T(8,128)(2,1)S(1)} %copy-done.25), channel_id=1, replica_groups=mesh['section'=4,'coil'=4,'cuts'=2] {'section'}, dimensions={0}, use_global_device_ids=true | all-gather | bytes 23040 | tf_op jit(solution)/shard_map/all_gather | solution.py:245
  108.1 11.3 %fusion.22 = bf16[8,40,128,18]{2,3,1,0:T(8,128)(2,1)} fusion(f32[128]{0:T(128)S(1)} %get-tuple-element.76, bf16[8,40,18,128]{3,1,2,0:T(8,128)(2,1)} %bitcast.655, bf16[4,18,128]{2,1,0:T(8,128)(2,1)S(1)} %all_gather.28, bf16[4,128,18]{1,2,0:T(8,128)(2,1)S(1)} %all_gather.26), kind=kOutput, calls=%fused_computation.51 | convolution fusion | flops 408944640 | bytes 2961920 | tf_op jit(solution)/shard_map/fh,xyhz->xyfz/dot_general | solution.py:147
  139.6 8.6 %collective-permute-done.10 = bf16[8,80,2,128]{3,1,2,0:T(8,128)(2,1)S(1)} collective-permute-done((bf16[8,80,2,128]{3,1,2,0:T(8,128)(2,1)S(1)}, bf16[8,80,2,128]{3,1,2,0:T(8,128)(2,1)S(1)}, u32[]{:S(2)}, u32[]{:S(2)}) %collective-permute-start.10) | collective-permute-done | bytes 327712 | tf_op jit(solution)/shard_map/ppermute | solution.py:14
  152.6 8.9 %collective-permute-done.11 = bf16[8,80,2,128]{3,1,2,0:T(8,128)(2,1)S(1)} collective-permute-done((bf16[8,80,2,128]{3,1,2,0:T(8,128)(2,1)S(1)}, bf16[8,80,2,128]{3,1,2,0:T(8,128)(2,1)S(1)}, u32[]{:S(2)}, u32[]{:S(2)}) %collective-permute-start.11) | collective-permute-done | bytes 327712 | tf_op jit(solution)/shard_map/ppermute | solution.py:14
  165.9 7.4 %collective-permute-done.13 = bf16[16,40,2,128]{3,1,0,2:T(8,128)(2,1)S(1)} collective-permute-done((bf16[16,40,2,128]{3,1,0,2:T(8,128)(2,1)S(1)}, bf16[16,40,2,128]{3,1,0,2:T(8,128)(2,1)S(1)}, u32[]{:S(2)}, u32[]{:S(2)}) %collective-permute-start.13) | collective-permute-done | bytes 327712 | tf_op jit(solution)/shard_map/ppermute | solution.py:41
  194.1 22.8 %reduce-scatter.13.cloned.1.call-done = bf16[8,80,2,128]{3,1,2,0:T(8,128)(2,1)} async-done(((bf16[32,80,2,128]{3,1,2,0:T(8,128)(2,1)}), bf16[8,80,2,128]{3,1,2,0:T(8,128)(2,1)}) %reduce-scatter.13.cloned.1.call-update) | async-done | bytes 327696 | tf_op jit(solution)/shard_map/reduce_scatter | solution.py:157
  219.3 11.3 %fusion.20 = bf16[8,40,128,18]{2,3,1,0:T(8,128)(2,1)} fusion(f32[128]{0:T(128)S(1)} %copy-done.28, bf16[8,40,18,128]{3,1,2,0:T(8,128)(2,1)} %bitcast.656, bf16[4,18,128]{2,1,0:T(8,128)(2,1)S(1)} %all_gather.28, bf16[4,128,18]{1,2,0:T(8,128)(2,1)S(1)} %all_gather.26), kind=kOutput, calls=%fused_computation.50 | convolution fusion | flops 408944640 | bytes 2961920 | tf_op jit(solution)/shard_map/fh,xyhz->xyfz/dot_general | solution.py:147
  250.2 8.6 %collective-permute-done.20 = bf16[8,80,2,128]{3,1,2,0:T(8,128)(2,1)S(1)} collective-permute-done((bf16[8,80,2,128]{3,1,2,0:T(8,128)(2,1)S(1)}, bf16[8,80,2,128]{3,1,2,0:T(8,128)(2,1)S(1)}, u32[]{:S(2)}, u32[]{:S(2)}) %collective-permute-start.20) | collective-permute-done | bytes 327712 | tf_op jit(solution)/shard_map/ppermute | solution.py:14
  263.1 8.9 %collective-permute-done.21 = bf16[8,80,2,128]{3,1,2,0:T(8,128)(2,1)S(1)} collective-permute-done((bf16[8,80,2,128]{3,1,2,0:T(8,128)(2,1)S(1)}, bf16[8,80,2,128]{3,1,2,0:T(8,128)(2,1)S(1)}, u32[]{:S(2)}, u32[]{:S(2)}) %collective-permute-start.21) | collective-permute-done | bytes 327712 | tf_op jit(solution)/shard_map/ppermute | solution.py:14
  276.3 7.4 %collective-permute-done.23 = bf16[16,40,2,128]{3,1,0,2:T(8,128)(2,1)S(1)} collective-permute-done((bf16[16,40,2,128]{3,1,0,2:T(8,128)(2,1)S(1)}, bf16[16,40,2,128]{3,1,0,2:T(8,128)(2,1)S(1)}, u32[]{:S(2)}, u32[]{:S(2)}) %collective-permute-start.23) | collective-permute-done | bytes 327712 | tf_op jit(solution)/shard_map/ppermute | solution.py:41
  304.5 22.6 %reduce-scatter.17.cloned.1.call-done = bf16[8,80,2,128]{3,1,2,0:T(8,128)(2,1)} async-done(((bf16[32,80,2,128]{3,1,2,0:T(8,128)(2,1)}), bf16[8,80,2,128]{3,1,2,0:T(8,128)(2,1)}) %reduce-scatter.17.cloned.1.call-update) | async-done | bytes 327696 | tf_op jit(solution)/shard_map/reduce_scatter | solution.py:157
  329.2 11.3 %fusion.18 = bf16[8,40,128,18]{2,3,1,0:T(8,128)(2,1)} fusion(f32[128]{0:T(128)S(1)} %copy-done.27, bf16[8,40,18,128]{3,1,2,0:T(8,128)(2,1)} %bitcast.657, bf16[4,18,128]{2,1,0:T(8,128)(2,1)S(1)} %all_gather.28, bf16[4,128,18]{1,2,0:T(8,128)(2,1)S(1)} %all_gather.26), kind=kOutput, calls=%fused_computation.49 | convolution fusion | flops 408944640 | bytes 2961920 | tf_op jit(solution)/shard_map/fh,xyhz->xyfz/dot_general | solution.py:147
  360.1 8.6 %collective-permute-done.30 = bf16[8,80,2,128]{3,1,2,0:T(8,128)(2,1)S(1)} collective-permute-done((bf16[8,80,2,128]{3,1,2,0:T(8,128)(2,1)S(1)}, bf16[8,80,2,128]{3,1,2,0:T(8,128)(2,1)S(1)}, u32[]{:S(2)}, u32[]{:S(2)}) %collective-permute-start.30) | collective-permute-done | bytes 327712 | tf_op jit(solution)/shard_map/ppermute | solution.py:14
  373.0 8.9 %collective-permute-done.31 = bf16[8,80,2,128]{3,1,2,0:T(8,128)(2,1)S(1)} collective-permute-done((bf16[8,80,2,128]{3,1,2,0:T(8,128)(2,1)S(1)}, bf16[8,80,2,128]{3,1,2,0:T(8,128)(2,1)S(1)}, u32[]{:S(2)}, u32[]{:S(2)}) %collective-permute-start.31) | collective-permute-done | bytes 327712 | tf_op jit(solution)/shard_map/ppermute | solution.py:14
  386.4 7.5 %collective-permute-done.33 = bf16[16,40,2,128]{3,1,0,2:T(8,128)(2,1)S(1)} collective-permute-done((bf16[16,40,2,128]{3,1,0,2:T(8,128)(2,1)S(1)}, bf16[16,40,2,128]{3,1,0,2:T(8,128)(2,1)S(1)}, u32[]{:S(2)}, u32[]{:S(2)}) %collective-permute-start.33) | collective-permute-done | bytes 327712 | tf_op jit(solution)/shard_map/ppermute | solution.py:41
  396.7 6.6 %collective-permute-done.34 = bf16[16,40,2,128]{3,1,0,2:T(8,128)(2,1)S(1)} collective-permute-done((bf16[16,40,2,128]{3,1,0,2:T(8,128)(2,1)S(1)}, bf16[16,40,2,128]{3,1,0,2:T(8,128)(2,1)S(1)}, u32[]{:S(2)}, u32[]{:S(2)}) %collective-permute-start.34) | collective-permute-done | bytes 327712 | tf_op jit(solution)/shard_map/ppermute | solution.py:41
  414.6 22.6 %reduce-scatter.21.cloned.1.call-done = bf16[8,80,2,128]{3,1,2,0:T(8,128)(2,1)} async-done(((bf16[32,80,2,128]{3,1,2,0:T(8,128)(2,1)}), bf16[8,80,2,128]{3,1,2,0:T(8,128)(2,1)}) %reduce-scatter.21.cloned.1.call-update) | async-done | bytes 327696 | tf_op jit(solution)/shard_map/reduce_scatter | solution.py:157
  439.1 11.3 %fusion.16 = bf16[8,40,128,18]{2,3,1,0:T(8,128)(2,1)} fusion(f32[128]{0:T(128)S(1)} %get-tuple-element.79, bf16[8,40,18,128]{3,1,2,0:T(8,128)(2,1)} %bitcast.654, bf16[4,18,128]{2,1,0:T(8,128)(2,1)} %copy-done.19, bf16[4,128,18]{1,2,0:T(8,128)(2,1)S(1)} %all_gather.26), kind=kOutput, calls=%fused_computation.48 | convolution fusion | flops 408944640 | bytes 2961920 | tf_op jit(solution)/shard_map/fh,xyhz->xyfz/dot_general | solution.py:147
  464.7 13.8 %all_to_all.12 = bf16[4,1,8,40,2,128]{5,4,3,2,1,0:T(2,128)(2,1)S(1)} all-to-all(bf16[4,1,8,40,2,128]{5,4,3,2,1,0:T(2,128)(2,1)S(1)} %copy.365), channel_id=1, replica_groups=mesh['section'=4,'coil'=4,'cuts'=2] {'section'}, dimensions={0} | all-to-all | bytes 1310720 | tf_op jit(solution)/shard_map/all_to_all | solution.py:268
  (350 shorter events, 207.6 us)
Async XLA Ops:
  6.5 99.6 %reduce-scatter.9.cloned.1.call-start = ((), (), s32[]{:S(2)}) async-start(), calls=%async_computation.9 | async-start | bytes 1638400 | tf_op jit(solution)/shard_map/reduce_scatter | solution.py:157
  9.9 22.5 %collective-permute-start.2 = (bf16[8,80,2,128]{3,1,2,0:T(8,128)(2,1)S(1)}, bf16[8,80,2,128]{3,1,2,0:T(8,128)(2,1)}, u32[]{:S(2)}, u32[]{:S(2)}) collective-permute-start(bf16[8,80,2,128]{3,1,2,0:T(8,128)(2,1)S(1)} %bitcast.658), channel_id=1, source_target_pairs={{0,6},{2,0},{4,2},{6,4},{1,7},{3,1},{5,3},{7,5},{8,14},{10,8},{12,... | collective-permute-start | bytes 983048 | tf_op jit(solution)/shard_map/ppermute | solution.py:16
  14.9 15.3 %collective-permute-start = (bf16[8,80,2,128]{3,1,2,0:T(8,128)(2,1)S(1)}, bf16[8,80,2,128]{3,1,2,0:T(8,128)(2,1)}, u32[]{:S(2)}, u32[]{:S(2)}) collective-permute-start(bf16[8,80,2,128]{3,1,2,0:T(8,128)(2,1)S(1)} %bitcast.659), channel_id=1, source_target_pairs={{0,2},{2,4},{4,6},{6,0},{1,3},{3,5},{5,7},{7,1},{8,10},{10,12},{12... | collective-permute-start | bytes 983048 | tf_op jit(solution)/shard_map/ppermute | solution.py:14
  30.2 10.9 %collective-permute-start.1 = (bf16[8,80,2,128]{3,1,2,0:T(8,128)(2,1)}, bf16[8,80,2,128]{3,1,2,0:T(8,128)(2,1)S(1)}, u32[]{:S(2)}, u32[]{:S(2)}) collective-permute-start(bf16[8,80,2,128]{3,1,2,0:T(8,128)(2,1)} %collective-permute-done), channel_id=1, source_target_pairs={{0,2},{2,4},{4,6},{6,0},{1,3},{3,5},{5,7},{7,1},{8,10},{10,12},{12... | collective-permute-start | bytes 983048 | tf_op jit(solution)/shard_map/ppermute | solution.py:14
  65.8 58.7 %reduce-scatter.11.cloned.1.call-start = ((), (), s32[]{:S(2)}) async-start(), calls=%async_computation.10 | async-start | bytes 491520 | tf_op jit(solution)/shard_map/reduce_scatter | solution.py:163
  65.9 37.6 %collective-permute-start.6 = (bf16[8,1,2,128]{3,1,2,0:T(2,128)(2,1)S(1)}, bf16[8,1,2,128]{3,1,2,0:T(2,128)(2,1)S(1)}, u32[]{:S(2)}, u32[]{:S(2)}) collective-permute-start(bf16[8,1,2,128]{3,1,2,0:T(2,128)(2,1)S(1)} %get-tuple-element.70), channel_id=1, source_target_pairs={{0,1},{2,3},{4,5},{6,7},{8,9},{10,11},{12,13},{14,15},{16,17},{18,... | collective-permute-start | bytes 12296 | tf_op jit(solution)/shard_map/ppermute | solution.py:28
  67.2 36.3 %collective-permute-start.7 = (bf16[8,1,2,128]{3,1,2,0:T(2,128)(2,1)S(1)}, bf16[8,1,2,128]{3,1,2,0:T(2,128)(2,1)S(1)}, u32[]{:S(2)}, u32[]{:S(2)}) collective-permute-start(bf16[8,1,2,128]{3,1,2,0:T(2,128)(2,1)S(1)} %get-tuple-element.71), channel_id=1, source_target_pairs={{1,0},{3,2},{5,4},{7,6},{9,8},{11,10},{13,12},{15,14},{17,16},{19,... | collective-permute-start | bytes 12296 | tf_op jit(solution)/shard_map/ppermute | solution.py:29
  108.0 108.9 %reduce-scatter.13.cloned.1.call-start = ((), (), s32[]{:S(2)}) async-start(), calls=%async_computation.11 | async-start | bytes 1638400 | tf_op jit(solution)/shard_map/reduce_scatter | solution.py:157
  135.8 12.4 %collective-permute-start.10 = (bf16[8,80,2,128]{3,1,2,0:T(8,128)(2,1)S(1)}, bf16[8,80,2,128]{3,1,2,0:T(8,128)(2,1)S(1)}, u32[]{:S(2)}, u32[]{:S(2)}) collective-permute-start(bf16[8,80,2,128]{3,1,2,0:T(8,128)(2,1)S(1)} %all_gather.29), channel_id=1, source_target_pairs={{0,2},{2,4},{4,6},{6,0},{1,3},{3,5},{5,7},{7,1},{8,10},{10,12},{12... | collective-permute-start | bytes 983048 | tf_op jit(solution)/shard_map/ppermute | solution.py:14
  135.8 16.8 %collective-permute-start.12 = (bf16[8,80,2,128]{3,1,2,0:T(8,128)(2,1)S(1)}, bf16[8,80,2,128]{3,1,2,0:T(8,128)(2,1)S(1)}, u32[]{:S(2)}, u32[]{:S(2)}) collective-permute-start(bf16[8,80,2,128]{3,1,2,0:T(8,128)(2,1)S(1)} %all_gather.29), channel_id=1, source_target_pairs={{0,6},{2,0},{4,2},{6,4},{1,7},{3,1},{5,3},{7,5},{8,14},{10,8},{12,... | collective-permute-start | bytes 983048 | tf_op jit(solution)/shard_map/ppermute | solution.py:16
  148.2 13.2 %collective-permute-start.11 = (bf16[8,80,2,128]{3,1,2,0:T(8,128)(2,1)S(1)}, bf16[8,80,2,128]{3,1,2,0:T(8,128)(2,1)S(1)}, u32[]{:S(2)}, u32[]{:S(2)}) collective-permute-start(bf16[8,80,2,128]{3,1,2,0:T(8,128)(2,1)S(1)} %collective-permute-done.10), channel_id=1, source_target_pairs={{0,2},{2,4},{4,6},{6,0},{1,3},{3,5},{5,7},{7,1},{8,10},{10,12},{12... | collective-permute-start | bytes 983048 | tf_op jit(solution)/shard_map/ppermute | solution.py:14
  164.4 9.0 %collective-permute-start.13 = (bf16[16,40,2,128]{3,1,0,2:T(8,128)(2,1)S(1)}, bf16[16,40,2,128]{3,1,0,2:T(8,128)(2,1)S(1)}, u32[]{:S(2)}, u32[]{:S(2)}) collective-permute-start(bf16[16,40,2,128]{3,1,0,2:T(8,128)(2,1)S(1)} %dynamic-slice_bitcast_fusion.5), channel_id=1, source_target_pairs={{0,8},{8,0},{16,24},{24,16},{1,9},{9,1},{17,25},{25,17},{2,10},{10... | collective-permute-start | bytes 983048 | tf_op jit(solution)/shard_map/ppermute | solution.py:41
  187.0 48.1 %reduce-scatter.15.cloned.1.call-start = ((), (), s32[]{:S(2)}) async-start(), calls=%async_computation.12 | async-start | bytes 491520 | tf_op jit(solution)/shard_map/reduce_scatter | solution.py:163
  218.7 108.3 %reduce-scatter.17.cloned.1.call-start = ((), (), s32[]{:S(2)}) async-start(), calls=%async_computation.13 | async-start | bytes 1638400 | tf_op jit(solution)/shard_map/reduce_scatter | solution.py:157
  246.3 12.4 %collective-permute-start.20 = (bf16[8,80,2,128]{3,1,2,0:T(8,128)(2,1)S(1)}, bf16[8,80,2,128]{3,1,2,0:T(8,128)(2,1)S(1)}, u32[]{:S(2)}, u32[]{:S(2)}) collective-permute-start(bf16[8,80,2,128]{3,1,2,0:T(8,128)(2,1)S(1)} %all_gather.30), channel_id=1, source_target_pairs={{0,2},{2,4},{4,6},{6,0},{1,3},{3,5},{5,7},{7,1},{8,10},{10,12},{12... | collective-permute-start | bytes 983048 | tf_op jit(solution)/shard_map/ppermute | solution.py:14
  246.3 16.8 %collective-permute-start.22 = (bf16[8,80,2,128]{3,1,2,0:T(8,128)(2,1)S(1)}, bf16[8,80,2,128]{3,1,2,0:T(8,128)(2,1)S(1)}, u32[]{:S(2)}, u32[]{:S(2)}) collective-permute-start(bf16[8,80,2,128]{3,1,2,0:T(8,128)(2,1)S(1)} %all_gather.30), channel_id=1, source_target_pairs={{0,6},{2,0},{4,2},{6,4},{1,7},{3,1},{5,3},{7,5},{8,14},{10,8},{12,... | collective-permute-start | bytes 983048 | tf_op jit(solution)/shard_map/ppermute | solution.py:16
  258.8 13.2 %collective-permute-start.21 = (bf16[8,80,2,128]{3,1,2,0:T(8,128)(2,1)S(1)}, bf16[8,80,2,128]{3,1,2,0:T(8,128)(2,1)S(1)}, u32[]{:S(2)}, u32[]{:S(2)}) collective-permute-start(bf16[8,80,2,128]{3,1,2,0:T(8,128)(2,1)S(1)} %collective-permute-done.20), channel_id=1, source_target_pairs={{0,2},{2,4},{4,6},{6,0},{1,3},{3,5},{5,7},{7,1},{8,10},{10,12},{12... | collective-permute-start | bytes 983048 | tf_op jit(solution)/shard_map/ppermute | solution.py:14
  297.4 47.7 %reduce-scatter.19.cloned.1.call-start = ((), (), s32[]{:S(2)}) async-start(), calls=%async_computation.14 | async-start | bytes 491520 | tf_op jit(solution)/shard_map/reduce_scatter | solution.py:163
  328.9 108.3 %reduce-scatter.21.cloned.1.call-start = ((), (), s32[]{:S(2)}) async-start(), calls=%async_computation.15 | async-start | bytes 1638400 | tf_op jit(solution)/shard_map/reduce_scatter | solution.py:157
  356.3 12.4 %collective-permute-start.30 = (bf16[8,80,2,128]{3,1,2,0:T(8,128)(2,1)S(1)}, bf16[8,80,2,128]{3,1,2,0:T(8,128)(2,1)S(1)}, u32[]{:S(2)}, u32[]{:S(2)}) collective-permute-start(bf16[8,80,2,128]{3,1,2,0:T(8,128)(2,1)S(1)} %all_gather.31), channel_id=1, source_target_pairs={{0,2},{2,4},{4,6},{6,0},{1,3},{3,5},{5,7},{7,1},{8,10},{10,12},{12... | collective-permute-start | bytes 983048 | tf_op jit(solution)/shard_map/ppermute | solution.py:14
  356.3 16.8 %collective-permute-start.32 = (bf16[8,80,2,128]{3,1,2,0:T(8,128)(2,1)S(1)}, bf16[8,80,2,128]{3,1,2,0:T(8,128)(2,1)S(1)}, u32[]{:S(2)}, u32[]{:S(2)}) collective-permute-start(bf16[8,80,2,128]{3,1,2,0:T(8,128)(2,1)S(1)} %all_gather.31), channel_id=1, source_target_pairs={{0,6},{2,0},{4,2},{6,4},{1,7},{3,1},{5,3},{7,5},{8,14},{10,8},{12,... | collective-permute-start | bytes 983048 | tf_op jit(solution)/shard_map/ppermute | solution.py:16
  368.7 13.2 %collective-permute-start.31 = (bf16[8,80,2,128]{3,1,2,0:T(8,128)(2,1)S(1)}, bf16[8,80,2,128]{3,1,2,0:T(8,128)(2,1)S(1)}, u32[]{:S(2)}, u32[]{:S(2)}) collective-permute-start(bf16[8,80,2,128]{3,1,2,0:T(8,128)(2,1)S(1)} %collective-permute-done.30), channel_id=1, source_target_pairs={{0,2},{2,4},{4,6},{6,0},{1,3},{3,5},{5,7},{7,1},{8,10},{10,12},{12... | collective-permute-start | bytes 983048 | tf_op jit(solution)/shard_map/ppermute | solution.py:14
  384.9 9.0 %collective-permute-start.33 = (bf16[16,40,2,128]{3,1,0,2:T(8,128)(2,1)S(1)}, bf16[16,40,2,128]{3,1,0,2:T(8,128)(2,1)S(1)}, u32[]{:S(2)}, u32[]{:S(2)}) collective-permute-start(bf16[16,40,2,128]{3,1,0,2:T(8,128)(2,1)S(1)} %dynamic-slice_bitcast_fusion.1), channel_id=1, source_target_pairs={{0,8},{8,0},{16,24},{24,16},{1,9},{9,1},{17,25},{25,17},{2,10},{10... | collective-permute-start | bytes 983048 | tf_op jit(solution)/shard_map/ppermute | solution.py:41
  407.6 47.3 %reduce-scatter.23.cloned.1.call-start = ((), (), s32[]{:S(2)}) async-start(), calls=%async_computation.16 | async-start | bytes 491520 | tf_op jit(solution)/shard_map/reduce_scatter | solution.py:163
  (54 other events, 1321.3 us)
Sparse Core Ops, SparseCore 0:
  65.9 29.5 reduce-scatter.8
  108.1 4.9 reduce-scatter.10
  187.1 29.7 reduce-scatter.12
  219.0 6.4 reduce-scatter.14
  297.5 29.4 reduce-scatter.16
  329.2 6.4 reduce-scatter.18
  407.7 29.4 reduce-scatter.20
  439.5 6.4 reduce-scatter.22
